TPU v7x, 256 devices: a whole 4x4x8 slice. The times are simulated.
256 devices in a mesh: member: 32 (over x, y, core), grid: 8 (over z).
Axes of the slice: x: 4, y: 4, z: 8, core: 2. Of those that a mesh axis runs over, the one named last changes fastest.
Arguments:
- prior_ensemble: bfloat16 [512, 48, 32768], P('member', None, 'grid'), may hold values from -6 to 6
- measured_location: int32 [8, 32, 128], P('grid', 'member'), may hold values from 0 to 6143
- measured_tally: int32 [8, 32], P('grid', 'member'), may hold values from 32 to 128, as said below
- measured_reading: float32 [8, 32, 128], P('grid', 'member'), may hold values from -6 to 6
- measured_noise_sigma: float32 [8, 32, 128], P('grid', 'member'), may hold values from 0.5 to 20, as said below
Outputs:
- analysis: bfloat16 [512, 48, 32768], P('member', None, 'grid')
Inputs may be any that keep to these rules, and one draw needn't show every extreme that they name: `measured_location`: cell of the observation within its block of 48 rows and 128 columns. `measured_tally`: some block in every draw uses all 128 slots. `measured_noise_sigma`: positive error deviations.
All inputs are finite; a program needn't handle non-finite values.
Results may differ from a plain program's by a relative error of at most 0.0058.
Values may be sent and summed in bfloat16 or wider, within the bound.
A program may use at most 128 MiB of HBM per device.

v0:
```python
import jax
import jax.numpy as jnp
from jax import lax
from jax.sharding import PartitionSpec as P

HIGHEST_PRECISION = lax.Precision.HIGHEST


def whiten(hx_values, values, errors, obs_total):
    hx_float = hx_values.astype(jnp.float32)
    hx_mean = jnp.mean(hx_float, axis=0)
    usable = (jnp.arange(hx_values.shape[1], dtype=jnp.int32) < obs_total).astype(jnp.float32)
    scale_obs = usable / errors
    whitened = (hx_float - hx_mean) * scale_obs
    innovation = (values - hx_mean) * scale_obs
    return (whitened, innovation)


def transform_matrix(gram_total, drive_vector):
    members = gram_total.shape[0]
    identity = jnp.eye(members, dtype=jnp.float32)
    system = (members - 1.0) * identity + gram_total
    factor_low = jnp.linalg.cholesky(system)
    inverse = jax.scipy.linalg.solve_triangular(factor_low, identity, lower=True)
    inner = jnp.dot(inverse, drive_vector, precision=HIGHEST_PRECISION)
    mean_weight = jnp.dot(inverse.T, inner, precision=HIGHEST_PRECISION)
    spread = jnp.sqrt(members - 1.0) * inverse.T
    return (mean_weight[:, None] + spread).astype(jnp.bfloat16)


def local_sums(whitened, innovation):
    gram_local = lax.dot_general(
        whitened, whitened, (((1,), (1,)), ((), ())), precision=HIGHEST_PRECISION
    )
    drive_local = jnp.dot(whitened, innovation, precision=HIGHEST_PRECISION)
    return (gram_local, drive_local)


def reduce_gram(whitened, innovation):
    gram_local, drive_local = local_sums(whitened, innovation)
    gram_total, drive_vector = lax.psum((gram_local, drive_local), ("member", "grid"))
    return transform_matrix(gram_total, drive_vector)


def apply_block(state_block, transform):
    members, row_count, columns = state_block.shape
    flattened = state_block.reshape(members, row_count * columns)
    state_mean = jnp.mean(flattened.astype(jnp.float32), axis=0)
    anomalies = (flattened.astype(jnp.float32) - state_mean).astype(jnp.bfloat16)
    increment = lax.dot_general(
        transform, anomalies, (((0,), (0,)), ((), ())), preferred_element_type=jnp.float32
    )
    return (state_mean + increment).astype(jnp.bfloat16).reshape(members, row_count, columns)


def local(
    prior_ensemble, measured_location, measured_tally, measured_reading, measured_noise_sigma
):
    values = measured_reading[0, 0]
    errors = measured_noise_sigma[0, 0]
    obs_total = measured_tally[0, 0]
    shard_profiles = lax.all_to_all(
        prior_ensemble, "member", split_axis=2, concat_axis=0, tiled=True
    )
    members, row_count, columns = shard_profiles.shape
    hx_values = jnp.take(
        shard_profiles.reshape(members, row_count * columns), measured_location[0, 0], axis=1
    )
    whitened, innovation = whiten(hx_values, values, errors, obs_total)
    transform = reduce_gram(whitened, innovation)
    updated = apply_block(shard_profiles, transform)
    return lax.all_to_all(updated, "member", split_axis=0, concat_axis=2, tiled=True)


def solution(mesh):
    in_specs = (
        P("member", None, "grid"),
        P("grid", "member", None),
        P("grid", "member"),
        P("grid", "member", None),
        P("grid", "member", None),
    )
    out_specs = P("member", None, "grid")
    return jax.shard_map(local, mesh=mesh, in_specs=in_specs, out_specs=out_specs, check_vma=False)
```

profile of v0, /device:TPU:1, one launch (start us, length us, event | category | flops | bytes accessed | tf_op | source)
XLA Modules:
  0.0 763.0 jit_solution(7519993507879228197)
XLA Ops:
  6.5 19.4 %copy.19 = bf16[16,48,4096]{1,0,2:T(8,128)(2,1)} copy(bf16[16,48,4096]{2,1,0:T(8,128)(2,1)} %param.5) | data formatting | bytes 12582912 | tf_op args[0]
  25.9 31.8 %reshape.139 = bf16[32,2,49152]{2,1,0:T(2,128)(2,1)} reshape(bf16[4096,16,48]{2,1,0:T(8,128)(2,1)} %bitcast.111) | data formatting | bytes 12582912
  57.7 8.8 %all-to-all-start = ((bf16[32,2,49152]{2,1,0:T(2,128)(2,1)}), bf16[32,2,49152]{2,1,0:T(2,128)(2,1)}, u32[]{:S(2)}, u32[]{:S(2)}) async-start(bf16[32,2,49152]{2,1,0:T(2,128)(2,1)} %reshape.139), calls=%async_computation | async-start | bytes 12582912 | tf_op jit(solution)/shard_map/all_to_all | solution.py:62
  68.9 74.8 %all-to-all-done = bf16[32,2,49152]{2,1,0:T(2,128)(2,1)} async-done(((bf16[32,2,49152]{2,1,0:T(2,128)(2,1)}), bf16[32,2,49152]{2,1,0:T(2,128)(2,1)}, u32[]{:S(2)}, u32[]{:S(2)}) %all-to-all-start) | async-done | bytes 6291488 | tf_op jit(solution)/shard_map/all_to_all | solution.py:62
  143.7 27.6 %reshape.140 = bf16[4096,16,48]{2,1,0:T(8,128)(2,1)} reshape(bf16[32,2,49152]{2,1,0:T(2,128)(2,1)} %all-to-all-done) | data formatting | bytes 12582912
  171.3 18.8 %copy.20 = bf16[16,48,32,128]{3,1,0,2:T(8,128)(2,1)} copy(bf16[16,48,32,128]{1,0,3,2:T(8,128)(2,1)} %bitcast.110) | data formatting | bytes 12582912 | tf_op jit(solution)/shard_map/all_to_all | solution.py:62
  190.1 7.1 copy.44
  197.1 8.7 %copy.21 = bf16[512,6144]{0,1:T(8,128)(2,1)} copy(bf16[512,6144]{1,0:T(8,128)(2,1)} %bitcast.119) | data formatting | bytes 12582912 | tf_op jit(solution)/shard_map/reshape | solution.py:47
  213.1 88.8 %psum.15 = f32[512]{0:T(512)S(1)} all-reduce(f32[512]{0:T(512)S(1)} %bitcast.121), channel_id=1, replica_groups=mesh['member'=32,'grid'=8] {'member','grid'}, use_global_device_ids=true, to_apply=%region_11.12 | all-reduce | flops 512 | bytes 4096 | tf_op jit(solution)/shard_map/psum | solution.py:41
  306.6 173.9 %all-reduce.3.cloned.1.call-done = f32[512,512]{0,1:T(8,128)} async-done(((f32[512,512]{0,1:T(8,128)}), f32[512,512]{0,1:T(8,128)}) %all-reduce.3.cloned.1.call-update) | async-done | bytes 1048592 | tf_op jit(solution)/shard_map/psum | solution.py:41
  483.6 11.7 %cholesky.107 = f32[128,128]{1,0:T(8,128)S(1)} custom-call(f32[128,128]{1,0:T(8,128)S(1)} %cholesky.269), custom_call_target="Cholesky" | custom-call | tf_op jit(solution)/shard_map/jit(cholesky)/cholesky | solution.py:23
  495.4 9.8 %custom-call.31 = f32[1,128,128]{1,2,0:T(8,128)S(1)} custom-call(f32[1,128,128]{2,1,0:T(8,128)S(1)} %get-tuple-element.36), custom_call_target="InvertDiagBlocksLowerTriangular" | custom-call | tf_op jit(solution)/shard_map/jit(cholesky)/cholesky | solution.py:23
  505.9 11.9 %cholesky.221 = f32[128,128]{1,0:T(8,128)S(1)} custom-call(f32[128,128]{1,0:T(8,128)S(1)} %cholesky.273), custom_call_target="Cholesky" | custom-call | tf_op jit(solution)/shard_map/jit(cholesky)/cholesky | solution.py:23
  518.1 9.8 %custom-call.32 = f32[1,128,128]{1,2,0:T(8,128)S(1)} custom-call(f32[1,128,128]{2,1,0:T(8,128)S(1)} %get-tuple-element.34), custom_call_target="InvertDiagBlocksLowerTriangular" | custom-call | tf_op jit(solution)/shard_map/jit(cholesky)/cholesky | solution.py:23
  530.7 13.2 %cholesky.242 = f32[128,128]{1,0:T(8,128)} custom-call(f32[128,128]{1,0:T(8,128)} %cholesky.278), custom_call_target="Cholesky" | custom-call | tf_op jit(solution)/shard_map/jit(cholesky)/cholesky | solution.py:23
  547.8 11.3 %custom-call.33 = f32[1,128,128]{1,2,0:T(8,128)} custom-call(f32[1,128,128]{2,1,0:T(8,128)} %get-tuple-element.32), custom_call_target="InvertDiagBlocksLowerTriangular" | custom-call | tf_op jit(solution)/shard_map/jit(cholesky)/cholesky | solution.py:23
  561.5 12.1 %cholesky.259 = f32[128,128]{1,0:T(8,128)S(1)} custom-call(f32[128,128]{1,0:T(8,128)S(1)} %convolution_subtract_fusion.5), custom_call_target="Cholesky" | custom-call | tf_op jit(solution)/shard_map/jit(cholesky)/cholesky | solution.py:23
  582.0 14.5 %while.1 = (s32[]{:T(128)}, f32[512,512]{0,1:T(8,128)}, s32[4,2]{0,1:T(2,128)S(1)}, f32[4,128,128]{2,1,0:T(8,128)}, s32[]{:T(128)}) while((s32[]{:T(128)}, f32[512,512]{0,1:T(8,128)}, s32[4,2]{0,1:T(2,128)S(1)}, f32[4,128,128]{2,1,0:T(8,128)}, s32[]{:T(128)}) %tuple.25), condition=%wide.while_cond, body=%wide.while_body.sunk | while | flops 2 | bytes 393829 | solution.py:24
  596.5 40.1 %custom-call.34 = f32[4,128,128]{1,2,0:T(8,128)S(1)} custom-call(f32[4,128,128]{2,1,0:T(8,128)} %get-tuple-element.12), custom_call_target="InvertDiagBlocksLowerTriangular" | custom-call | tf_op jit(solution)/shard_map/jit(_solve_triangular)/triangular_solve | solution.py:24
  646.3 6.7 fusion.1
  653.0 4.7 copy.38
  657.7 81.4 %all_to_all.33 = bf16[512,48,128]{2,1,0:T(8,128)(2,1)S(1)} all-to-all(bf16[512,48,128]{2,1,0:T(8,128)(2,1)S(1)} %bitcast.116), channel_id=1, replica_groups=mesh['member'=32,'grid'=8] {'member'}, dimensions={0} | all-to-all | bytes 12582912 | tf_op jit(solution)/shard_map/all_to_all | solution.py:72
  739.0 6.7 copy.45
  745.7 10.3 %all_to_all.30 = bf16[16,48,4096]{2,1,0:T(8,128)(2,1)} reshape(bf16[16,48,32,128]{3,2,1,0:T(8,128)(2,1)} %bitcast.118) | data formatting | bytes 12582912 | tf_op jit(solution)/shard_map/all_to_all | solution.py:72
  (92 shorter events, 56.9 us)
Async XLA Ops:
  57.6 10.1 %copy-start.3 = (s32[1,1,128]{2,1,0:T(1,128)S(1)}, s32[1,1,128]{2,1,0:T(1,128)}, u32[]{:S(2)}) copy-start(s32[1,1,128]{2,1,0:T(1,128)} %param.6) | copy-start | bytes 1540
  57.7 86.1 %all-to-all-start = ((bf16[32,2,49152]{2,1,0:T(2,128)(2,1)}), bf16[32,2,49152]{2,1,0:T(2,128)(2,1)}, u32[]{:S(2)}, u32[]{:S(2)}) async-start(bf16[32,2,49152]{2,1,0:T(2,128)(2,1)} %reshape.139), calls=%async_computation | async-start | bytes 12582912 | tf_op jit(solution)/shard_map/all_to_all | solution.py:62
  66.4 414.0 %all-reduce.3.cloned.1.call-start = ((), (), s32[]{:S(2)}) async-start(), calls=%async_computation.2 | async-start | bytes 2097152 | tf_op jit(solution)/shard_map/psum | solution.py:41
  197.1 13.3 %copy-start.2 = (f32[1,1,128]{2,1,0:T(1,128)S(1)}, f32[1,1,128]{2,1,0:T(1,128)}, u32[]{:S(2)}) copy-start(f32[1,1,128]{2,1,0:T(1,128)} %param.9) | copy-start | bytes 1540
  197.1 15.6 %copy-start.4 = (f32[1,1,128]{2,1,0:T(1,128)S(1)}, f32[1,1,128]{2,1,0:T(1,128)}, u32[]{:S(2)}) copy-start(f32[1,1,128]{2,1,0:T(1,128)} %param.8) | copy-start | bytes 1540
  483.6 44.5 %copy-start = (f32[512,512]{1,0:T(8,128)}, f32[512,512]{1,0:T(8,128)S(1)}, u32[]{:S(2)}) copy-start(f32[512,512]{1,0:T(8,128)S(1)} %fusion.6) | copy-start | bytes 3145732
  528.5 117.8 %slice-start = ((s8[6291456]{0:T(1024)(128)(4,1)}), s8[2097152]{0:T(1024)(128)(4,1)S(1)}, s32[]{:S(2)}) async-start(s8[6291456]{0:T(1024)(128)(4,1)} %bitcast.113), calls=%async_computation.3 | async-start | bytes 4194304
  580.2 66.1 %copy-start.1 = (f32[6144]{0:T(1024)S(1)}, f32[6144]{0:T(1024)}, u32[]{:S(2)}) copy-start(f32[6144]{0:T(1024)} %multiply_bitcast_fusion) | copy-start | bytes 73732
  638.6 7.7 %slice-start.1 = ((s8[6291456]{0:T(1024)(128)(4,1)}), s8[4194304]{0:T(1024)(128)(4,1)S(1)}, s32[]{:S(2)}) async-start(s8[6291456]{0:T(1024)(128)(4,1)} %bitcast.113), calls=%async_computation.4 | async-start | bytes 8388608
Sparse Core Ops, SparseCore 0:
  212.8 267.5 all-reduce.2
where the time goes:
time: 773 us; the launch traced here: 763 us
  waiting for transfers between devices  249 us (32%)
  blocking collectives  170 us (22%)
  local copies, waits for them, and re-layouts  158 us (20%)
  other arithmetic  136 us (18%)
  matrix products  23.9 us (3%)
  between operations  17.1 us (2%)
  starting transfers between devices  8.8 us (1%)
    psum x1, waiting for transfers between devices, reduce_gram(): lax.psum((gram_local, drive_local), ('member', 'grid'))  174 us
    unnamed x19, local copies, waits for them, and re-layouts  90.5 us
    psum x1, blocking collectives, reduce_gram(): lax.psum((gram_local, drive_local), ('member', 'grid'))  88.8 us
    another operation x15, other arithmetic, transform_matrix(): factor_low = jnp.linalg.cholesky(system)  85.3 us
    all_to_all x1, blocking collectives, local(): lax.all_to_all(updated, 'member', split_axis=0, concat_axis=2, tiled=True)  81.4 us
    all_to_all x1, waiting for transfers between devices, local(): lax.all_to_all(prior_ensemble, 'member', split_axis=2, concat_axis=0, til...  74.8 us
    another operation x3, other arithmetic, transform_matrix(): jax.scipy.linalg.solve_triangular(factor_low, identity, lower=True)  41.8 us
    all_to_all x1, local copies, waits for them, and re-layouts, local(): lax.all_to_all(prior_ensemble, 'member', split_axis=2, concat_axis=0, til...  18.8 us
  transfers between devices with their start and end apart: 2, of which 2 were waited for; matrix products, arithmetic and copies ran while one was open for 1% of the time, Pallas kernels for 0%

commit v1 on v0

--- a/solution.py
+++ b/solution.py
@@ -4,6 +4,13 @@
 from jax.sharding import PartitionSpec as P
 
 HIGHEST_PRECISION = lax.Precision.HIGHEST
+
+
+def stacked_exchange(block, mesh_axis, split, join):
+    devices = lax.axis_size(mesh_axis)
+    blocks = jnp.stack(jnp.split(block, devices, axis=split), axis=0)
+    blocks = lax.all_to_all(blocks, mesh_axis, split_axis=0, concat_axis=0)
+    return jnp.concatenate(blocks, axis=join)
 
 
 def whiten(hx_values, values, errors, obs_total):
@@ -69,7 +76,7 @@
     whitened, innovation = whiten(hx_values, values, errors, obs_total)
     transform = reduce_gram(whitened, innovation)
     updated = apply_block(shard_profiles, transform)
-    return lax.all_to_all(updated, "member", split_axis=0, concat_axis=2, tiled=True)
+    return stacked_exchange(updated, "member", 0, 2)
 
 
 def solution(mesh):

time: 773 us -> 756 us (0.978)
  local copies, waits for them, and re-layouts: 158 us -> 143 us
    all_to_all x2 -> x0, local copies, waits for them, and re-layouts: 17 us -> none  [local(): lax.all_to_all(updated, 'member', split_axis=0, concat_axis=2, tiled=True)]
    unnamed x19 -> x83, local copies, waits for them, and re-layouts: 90.5 us -> 88 us
where the time goes in v1:
time: 756 us; the launch traced here: 746 us
  waiting for transfers between devices  249 us (33%)
  blocking collectives  170 us (22%)
  local copies, waits for them, and re-layouts  143 us (19%)
  other arithmetic  136 us (18%)
  matrix products  22.3 us (3%)
  between operations  17.7 us (2%)
  starting transfers between devices  8.8 us (1%)
    psum x1, waiting for transfers between devices, reduce_gram(): lax.psum((gram_local, drive_local), ('member', 'grid'))  174 us
    psum x1, blocking collectives, reduce_gram(): lax.psum((gram_local, drive_local), ('member', 'grid'))  88.8 us
    unnamed x83, local copies, waits for them, and re-layouts  88 us
    another operation x15, other arithmetic, transform_matrix(): factor_low = jnp.linalg.cholesky(system)  85.2 us
    all_to_all x1, blocking collectives, stacked_exchange(): blocks = lax.all_to_all(blocks, mesh_axis, split_axis=0, concat_axis=0)  81.4 us
    all_to_all x1, waiting for transfers between devices, local(): lax.all_to_all(prior_ensemble, 'member', split_axis=2, concat_axis=0, til...  74.8 us
    another operation x3, other arithmetic, transform_matrix(): jax.scipy.linalg.solve_triangular(factor_low, identity, lower=True)  41.8 us
    all_to_all x1, local copies, waits for them, and re-layouts, local(): lax.all_to_all(prior_ensemble, 'member', split_axis=2, concat_axis=0, til...  18.8 us
  transfers between devices with their start and end apart: 2, of which 2 were waited for; matrix products, arithmetic and copies ran while one was open for 1% of the time, Pallas kernels for 0%

profile of v1, /device:TPU:1, one launch (start us, length us, event | category | flops | bytes accessed | tf_op | source)
XLA Modules:
  0.0 746.1 jit_solution(13497720181277325075)
XLA Ops:
  6.5 19.4 %copy.19 = bf16[16,48,4096]{1,0,2:T(8,128)(2,1)} copy(bf16[16,48,4096]{2,1,0:T(8,128)(2,1)} %param.5) | data formatting | bytes 12582912 | tf_op args[0]
  25.9 31.8 %reshape.208 = bf16[32,2,49152]{2,1,0:T(2,128)(2,1)} reshape(bf16[4096,16,48]{2,1,0:T(8,128)(2,1)} %bitcast.300) | data formatting | bytes 12582912
  57.7 8.8 %all-to-all-start = ((bf16[32,2,49152]{2,1,0:T(2,128)(2,1)}), bf16[32,2,49152]{2,1,0:T(2,128)(2,1)}, u32[]{:S(2)}, u32[]{:S(2)}) async-start(bf16[32,2,49152]{2,1,0:T(2,128)(2,1)} %reshape.208), calls=%async_computation | async-start | bytes 12582912 | tf_op jit(solution)/shard_map/all_to_all | solution.py:69
  68.9 74.8 %all-to-all-done = bf16[32,2,49152]{2,1,0:T(2,128)(2,1)} async-done(((bf16[32,2,49152]{2,1,0:T(2,128)(2,1)}), bf16[32,2,49152]{2,1,0:T(2,128)(2,1)}, u32[]{:S(2)}, u32[]{:S(2)}) %all-to-all-start) | async-done | bytes 6291488 | tf_op jit(solution)/shard_map/all_to_all | solution.py:69
  143.7 27.6 %reshape.209 = bf16[4096,16,48]{2,1,0:T(8,128)(2,1)} reshape(bf16[32,2,49152]{2,1,0:T(2,128)(2,1)} %all-to-all-done) | data formatting | bytes 12582912
  171.3 18.8 %copy.20 = bf16[16,48,32,128]{3,1,0,2:T(8,128)(2,1)} copy(bf16[16,48,32,128]{1,0,3,2:T(8,128)(2,1)} %bitcast.299) | data formatting | bytes 12582912 | tf_op jit(solution)/shard_map/all_to_all | solution.py:69
  190.1 7.1 copy.76
  197.1 8.7 %copy.21 = bf16[512,6144]{0,1:T(8,128)(2,1)} copy(bf16[512,6144]{1,0:T(8,128)(2,1)} %bitcast.305) | data formatting | bytes 12582912 | tf_op jit(solution)/shard_map/reshape | solution.py:54
  205.8 4.5 gather_fusion
  213.1 88.8 %psum.15 = f32[512]{0:T(512)S(1)} all-reduce(f32[512]{0:T(512)S(1)} %bitcast.339), channel_id=1, replica_groups=mesh['member'=32,'grid'=8] {'member','grid'}, use_global_device_ids=true, to_apply=%region_11.12 | all-reduce | flops 512 | bytes 4096 | tf_op jit(solution)/shard_map/psum | solution.py:48
  301.8 4.1 convert_reduce_fusion
  306.6 173.9 %all-reduce.3.cloned.1.call-done = f32[512,512]{0,1:T(8,128)} async-done(((f32[512,512]{0,1:T(8,128)}), f32[512,512]{0,1:T(8,128)}) %all-reduce.3.cloned.1.call-update) | async-done | bytes 1048592 | tf_op jit(solution)/shard_map/psum | solution.py:48
  483.6 11.7 %cholesky.107 = f32[128,128]{1,0:T(8,128)S(1)} custom-call(f32[128,128]{1,0:T(8,128)S(1)} %cholesky.269), custom_call_target="Cholesky" | custom-call | tf_op jit(solution)/shard_map/jit(cholesky)/cholesky | solution.py:30
  495.4 9.8 %custom-call.31 = f32[1,128,128]{1,2,0:T(8,128)S(1)} custom-call(f32[1,128,128]{2,1,0:T(8,128)S(1)} %get-tuple-element.68), custom_call_target="InvertDiagBlocksLowerTriangular" | custom-call | tf_op jit(solution)/shard_map/jit(cholesky)/cholesky | solution.py:30
  506.1 11.9 %cholesky.221 = f32[128,128]{1,0:T(8,128)S(1)} custom-call(f32[128,128]{1,0:T(8,128)S(1)} %cholesky.273), custom_call_target="Cholesky" | custom-call | tf_op jit(solution)/shard_map/jit(cholesky)/cholesky | solution.py:30
  518.1 9.8 %custom-call.32 = f32[1,128,128]{1,2,0:T(8,128)S(1)} custom-call(f32[1,128,128]{2,1,0:T(8,128)S(1)} %get-tuple-element.66), custom_call_target="InvertDiagBlocksLowerTriangular" | custom-call | tf_op jit(solution)/shard_map/jit(cholesky)/cholesky | solution.py:30
  530.7 13.2 %cholesky.242 = f32[128,128]{1,0:T(8,128)} custom-call(f32[128,128]{1,0:T(8,128)} %cholesky.278), custom_call_target="Cholesky" | custom-call | tf_op jit(solution)/shard_map/jit(cholesky)/cholesky | solution.py:30
  547.8 11.3 %custom-call.33 = f32[1,128,128]{1,2,0:T(8,128)} custom-call(f32[1,128,128]{2,1,0:T(8,128)} %get-tuple-element.64), custom_call_target="InvertDiagBlocksLowerTriangular" | custom-call | tf_op jit(solution)/shard_map/jit(cholesky)/cholesky | solution.py:30
  561.5 12.1 %cholesky.259 = f32[128,128]{1,0:T(8,128)S(1)} custom-call(f32[128,128]{1,0:T(8,128)S(1)} %convolution_subtract_fusion.5), custom_call_target="Cholesky" | custom-call | tf_op jit(solution)/shard_map/jit(cholesky)/cholesky | solution.py:30
  582.0 14.5 %while.1 = (s32[]{:T(128)}, f32[512,512]{0,1:T(8,128)}, s32[4,2]{0,1:T(2,128)S(1)}, f32[4,128,128]{2,1,0:T(8,128)}, s32[]{:T(128)}) while((s32[]{:T(128)}, f32[512,512]{0,1:T(8,128)}, s32[4,2]{0,1:T(2,128)S(1)}, f32[4,128,128]{2,1,0:T(8,128)}, s32[]{:T(128)}) %tuple.55), condition=%wide.while_cond, body=%wide.while_body.sunk | while | flops 2 | bytes 393829 | solution.py:31
  596.5 40.1 %custom-call.34 = f32[4,128,128]{1,2,0:T(8,128)S(1)} custom-call(f32[4,128,128]{2,1,0:T(8,128)} %get-tuple-element.12), custom_call_target="InvertDiagBlocksLowerTriangular" | custom-call | tf_op jit(solution)/shard_map/jit(_solve_triangular)/triangular_solve | solution.py:31
  646.3 5.0 add_convert_fusion
  654.1 81.4 %all_to_all.20 = bf16[32,16,48,128]{3,2,1,0:T(8,128)(2,1)S(1)} all-to-all(bf16[32,16,48,128]{3,2,1,0:T(8,128)(2,1)S(1)} %bitcast_dynamic-update-slice_fusion.1), channel_id=1, replica_groups=mesh['member'=32,'grid'=8] {'member'}, dimensions={0} | all-to-all | bytes 12582912 | tf_op jit(solution)/shard_map/all_to_all | solution.py:12
  735.5 3.6 copy_bitcast_fusion.1
  (156 shorter events, 50.5 us)
Async XLA Ops:
  57.6 10.1 %copy-start.3 = (s32[1,1,128]{2,1,0:T(1,128)S(1)}, s32[1,1,128]{2,1,0:T(1,128)}, u32[]{:S(2)}) copy-start(s32[1,1,128]{2,1,0:T(1,128)} %param.6) | copy-start | bytes 1540
  57.7 86.1 %all-to-all-start = ((bf16[32,2,49152]{2,1,0:T(2,128)(2,1)}), bf16[32,2,49152]{2,1,0:T(2,128)(2,1)}, u32[]{:S(2)}, u32[]{:S(2)}) async-start(bf16[32,2,49152]{2,1,0:T(2,128)(2,1)} %reshape.208), calls=%async_computation | async-start | bytes 12582912 | tf_op jit(solution)/shard_map/all_to_all | solution.py:69
  66.4 414.0 %all-reduce.3.cloned.1.call-start = ((), (), s32[]{:S(2)}) async-start(), calls=%async_computation.2 | async-start | bytes 2097152 | tf_op jit(solution)/shard_map/psum | solution.py:48
  197.1 13.3 %copy-start.2 = (f32[1,1,128]{2,1,0:T(1,128)S(1)}, f32[1,1,128]{2,1,0:T(1,128)}, u32[]{:S(2)}) copy-start(f32[1,1,128]{2,1,0:T(1,128)} %param.9) | copy-start | bytes 1540
  197.1 15.6 %copy-start.4 = (f32[1,1,128]{2,1,0:T(1,128)S(1)}, f32[1,1,128]{2,1,0:T(1,128)}, u32[]{:S(2)}) copy-start(f32[1,1,128]{2,1,0:T(1,128)} %param.8) | copy-start | bytes 1540
  483.6 44.5 %copy-start = (f32[512,512]{1,0:T(8,128)}, f32[512,512]{1,0:T(8,128)S(1)}, u32[]{:S(2)}) copy-start(f32[512,512]{1,0:T(8,128)S(1)} %fusion.5) | copy-start | bytes 3145732
  528.4 117.9 %slice-start = ((s8[6291456]{0:T(1024)(128)(4,1)}), s8[2097152]{0:T(1024)(128)(4,1)S(1)}, s32[]{:S(2)}) async-start(s8[6291456]{0:T(1024)(128)(4,1)} %bitcast.302), calls=%async_computation.3 | async-start | bytes 4194304
  580.2 66.1 %copy-start.1 = (f32[6144]{0:T(1024)S(1)}, f32[6144]{0:T(1024)}, u32[]{:S(2)}) copy-start(f32[6144]{0:T(1024)} %multiply_bitcast_fusion) | copy-start | bytes 73732
  638.5 7.8 %slice-start.1 = ((s8[6291456]{0:T(1024)(128)(4,1)}), s8[4194304]{0:T(1024)(128)(4,1)S(1)}, s32[]{:S(2)}) async-start(s8[6291456]{0:T(1024)(128)(4,1)} %bitcast.302), calls=%async_computation.4 | async-start | bytes 8388608
Sparse Core Ops, SparseCore 0:
  212.8 267.5 all-reduce.2
